TPU v7x, 256 devices: a whole 4x4x8 slice. The times are simulated.
256 devices in a mesh: expert: 64 (over y, x, z_lo), dp: 4 (over z_hi, core).
Axes of the slice: x: 4, y: 4, z: 8 (z_hi: 2, z_lo: 4; z = z_hi * 4 + z_lo), core: 2. Of those that a mesh axis runs over, the one named last changes fastest.
Arguments:
- tokens: bfloat16 [3072, 3584], P('expert'), may hold values from -6 to 6
- expert_weights: bfloat16 [64, 3, 3584, 1024], P('expert', None, None, 'dp'), may hold values from -0.09375 to 0.09375
- partner: int32 [64], replicated, may hold values from 0 to 63, as said below
- replica: int32 [64], replicated, may hold values from 0 to 63, as said below
- routing: int32 [3072, 8], P('expert'), may hold values from 0 to 127, all different within a row; in each aligned block of 48 rows (0 to 47, 48 to 95, ...) at most 6 rows name the same one
- gates: bfloat16 [3072, 8], P('expert'), may hold values from 0.099609375 to 1
Outputs:
- mixed: bfloat16 [3072, 3584], P('expert', 'dp')
Inputs may be any that keep to these rules, and one draw needn't show every extreme that they name: partner pairs devices: partner[partner[p]] = p; about half of the indices are paired with another, the rest with themselves. No expert appears more than 4 times in replica, and some expert appears exactly 4 times. `routing`: each row names 8 different slots; among the 48 rows of one device along expert no slot is named more than 6 times.
All inputs are finite; a program needn't handle non-finite values.
Results may differ from a plain program's by a relative error of at most 0.0058.
Values may be sent and summed in bfloat16 or wider, within the bound.
A program may use at most 128 MiB of HBM per device.

v0:
```python
import jax
import jax.numpy as jnp
from jax import lax
from jax.sharding import Mesh, PartitionSpec as P

GATHER_AXES = ("z_lo", "y", "x")
OWNER = ("y", "x", "z_lo")


def expert_hidden(packed, features, topk, hit, w):
    x = packed[:, :features]
    slots = packed[:, features : features + topk].astype(jnp.float32)
    weight = packed[:, features + topk : features + 2 * topk].astype(jnp.float32)
    ids = jnp.arange(hit.shape[0], dtype=jnp.float32)
    sel = jnp.sum(jnp.where((slots[:, :, None] == ids) & hit, weight[:, :, None], 0.0), axis=(1, 2))
    g = jnp.dot(x, w[0], preferred_element_type=jnp.float32)
    u = jnp.dot(x, w[1], preferred_element_type=jnp.float32)
    return ((jax.nn.silu(g) * u).astype(jnp.bfloat16), sel)


def down_project(h, sel, w_down):
    down = lax.dot_general(h, w_down, (((1,), (1,)), ((), ())), preferred_element_type=jnp.float32)
    return down * sel[:, None]


def shards(tokens, expert_weights, partner, replica, routing, gates):
    rows, features = tokens.shape
    topk = routing.shape[1]
    me = lax.axis_index(OWNER)
    core = lax.axis_index("core")
    half = rows // 2
    packed = jnp.concatenate(
        [
            tokens,
            routing.astype(jnp.bfloat16),
            gates,
            jnp.zeros((rows, 128 - 2 * topk), jnp.bfloat16),
        ],
        axis=1,
    )
    own = lax.dynamic_slice_in_dim(packed, core * half, half, axis=0)
    for axis in GATHER_AXES:
        own = lax.all_gather(own, axis, axis=0, tiled=True)
    other = lax.ppermute(own, "core", [(0, 1), (1, 0)])
    hit = jnp.stack([partner, replica], axis=1).reshape(-1) == me
    w = expert_weights[0]
    h_own, sel_own = expert_hidden(own, features, topk, hit, w)
    h_other, sel_other = expert_hidden(other, features, topk, hit, w)
    away = down_project(h_other, sel_other, w[2]).astype(jnp.bfloat16)
    returned = lax.ppermute(away, "core", [(0, 1), (1, 0)])
    total = (down_project(h_own, sel_own, w[2]) + returned.astype(jnp.float32)).astype(jnp.bfloat16)
    for axis in GATHER_AXES[::-1]:
        total = lax.psum_scatter(total, axis, scatter_dimension=0, tiled=True)
    total = lax.psum_scatter(total.astype(jnp.float32), "z_hi", scatter_dimension=1, tiled=True)
    return lax.all_to_all(
        total.astype(jnp.bfloat16), "core", split_axis=1, concat_axis=0, tiled=True
    )


def solution(mesh):
    grid = Mesh(mesh.devices.reshape(4, 4, 4, 2, 2), ("y", "x", "z_lo", "z_hi", "core"))
    dp = ("z_hi", "core")
    return jax.shard_map(
        shards,
        mesh=grid,
        in_specs=(
            P(OWNER, None),
            P(OWNER, None, None, dp),
            P(),
            P(),
            P(OWNER, None),
            P(OWNER, None),
        ),
        out_specs=P(OWNER, dp),
        check_vma=False,
    )
```

profile of v0, /device:TPU:1, one launch (start us, length us, event | category | flops | bytes accessed | tf_op | source)
XLA Modules:
  0.0 520.1 jit_solution(11850227993452138166)
XLA Ops:
  6.5 0.0 copy-start.1
  6.5 0.0 copy-start
  6.5 0.0 all-gather.3.cloned.1.call-start
  6.5 0.7 convert_element_type.36
  7.3 0.1 copy.19
  7.4 0.8 copy.20
  8.1 1.1 concatenate.3
  9.2 18.9 %all_gather.9 = bf16[96,3712]{1,0:T(8,128)(2,1)} all-gather(bf16[24,3712]{1,0:T(8,128)(2,1)S(1)} %constant_dynamic-slice_fusion), channel_id=1, replica_groups=mesh['y'=4,'x'=4,'z_lo'=4,'z_hi'=2,'core'=2] {'z_lo'}, dimensions={0}, use_global_device_ids=true | all-gather | bytes 890880 | tf_op jit(solution)/shard_map/all_gather | solution.py:43
  28.2 0.0 all-gather.3.cloned.1.call-update
  28.2 0.0 all-gather.5.cloned.1.call-start
  28.2 42.4 %all-gather.3.cloned.1.call-done = bf16[384,3712]{1,0:T(8,128)(2,1)} async-done(((bf16[96,3712]{1,0:T(8,128)(2,1)}), bf16[384,3712]{1,0:T(8,128)(2,1)}) %all-gather.3.cloned.1.call-update) | async-done | bytes 2850832 | tf_op jit(solution)/shard_map/all_gather | solution.py:43
  70.7 0.0 all-gather.5.cloned.1.call-update
  70.7 0.0 reduce-scatter.5.cloned.1.call-start
  70.8 113.1 %all-gather.5.cloned.1.call-done = bf16[1536,3712]{1,0:T(8,128)(2,1)} async-done(((bf16[384,3712]{1,0:T(8,128)(2,1)}), bf16[1536,3712]{1,0:T(8,128)(2,1)}) %all-gather.5.cloned.1.call-update) | async-done | bytes 11403280 | tf_op jit(solution)/shard_map/all_gather | solution.py:43
  183.8 0.7 collective-permute-start
  184.5 0.0 copy-done.1
  184.5 0.0 copy-done
  184.5 0.1 copy.21
  184.6 0.1 eq.44
  184.8 1.4 slice_convert_fusion.3
  186.2 15.7 %collective-permute-done = bf16[1536,3712]{1,0:T(8,128)(2,1)} collective-permute-done((bf16[1536,3712]{1,0:T(8,128)(2,1)}, bf16[1536,3712]{1,0:T(8,128)(2,1)}, u32[]{:S(2)}, u32[]{:S(2)}) %collective-permute-start) | collective-permute-done | bytes 11403296 | tf_op jit(solution)/shard_map/ppermute | solution.py:44
  202.0 1.3 slice_convert_fusion.1
  203.3 45.4 %select_reduce_fusion.1 = (f32[1536]{0:T(1024)S(1)}, f32[1536]{0:T(1024)S(1)}) fusion(f32[1536,8]{1,0:T(8,128)S(1)} %get-tuple-element.10, f32[1536,8]{1,0:T(8,128)S(1)} %get-tuple-element.9, pred[128]{0:T(512)(128)(4,1)S(1)} %eq.44, f32[1536,8]{1,0:T(8,128)S(1)} %get-tuple-element.8, f32[1536,8]{1,0:T(8,128)S(1)} %get-tuple-element.7), kind=kLoop, calls=%fused_computation.12 | loop fusion | flops 12579840 | bytes 209024 | tf_op jit(solution)/shard_map/reduce_sum | solution.py:15
  248.7 6.3 %fusion = f32[1536,256]{1,0:T(8,128)S(1)} fusion(bf16[1536,3712]{1,0:T(8,128)(2,1)} %collective-permute-done, bf16[1,3,3584,256]{3,2,1,0:T(8,128)(2,1)} %param.7), kind=kOutput, calls=%fused_computation.2 | convolution fusion | flops 2818572288 | bytes 14417920 | tf_op jit(solution)/shard_map/dot_general | solution.py:17
  255.0 17.7 %multiply_convert_fusion = bf16[1536,3584]{1,0:T(8,128)(2,1)} fusion(f32[1536]{0:T(1024)S(1)} %get-tuple-element.6, bf16[1,3,3584,256]{3,2,1,0:T(8,128)(2,1)} %param.7, f32[1536,256]{1,0:T(8,128)S(1)} %fusion, bf16[1536,3712]{1,0:T(8,128)(2,1)} %collective-permute-done), kind=kOutput, calls=%fused_computation.1 | convolution fusion | flops 5650513920 | bytes 27269120 | tf_op jit(solution)/shard_map/dot_general | solution.py:22
  272.7 0.4 collective-permute-start.1
  273.0 6.3 %fusion.6 = f32[1536,256]{1,0:T(8,128)S(1)} fusion(bf16[1536,3712]{1,0:T(8,128)(2,1)} %all-gather.5.cloned.1.call-done, bf16[1,3,3584,256]{3,2,1,0:T(8,128)(2,1)} %param.7), kind=kOutput, calls=%fused_computation.8 | convolution fusion | flops 2818572288 | bytes 14417920 | tf_op jit(solution)/shard_map/dot_general | solution.py:16
  279.4 10.5 %collective-permute-done.1 = bf16[1536,3584]{1,0:T(8,128)(2,1)} collective-permute-done((bf16[1536,3584]{1,0:T(8,128)(2,1)}, bf16[1536,3584]{1,0:T(8,128)(2,1)}, u32[]{:S(2)}, u32[]{:S(2)}) %collective-permute-start.1) | collective-permute-done | bytes 11010080 | tf_op jit(solution)/shard_map/ppermute | solution.py:50
  289.9 19.1 %add_convert_fusion = bf16[1536,3584]{1,0:T(8,128)(2,1)} fusion(bf16[1536,3584]{1,0:T(8,128)(2,1)} %collective-permute-done.1, f32[1536]{0:T(1024)S(1)} %get-tuple-element.5, bf16[1536,3712]{1,0:T(8,128)(2,1)} %all-gather.5.cloned.1.call-done, bf16[1,3,3584,256]{3,2,1,0:T(8,128)(2,1)} %param.7, f32[1536,256]{1,0:T(8,128)S(1)} %fusion.6), kind=kOutput, calls=%fused_computation | convolution fusion | flops 5661523968 | bytes 38279168 | tf_op jit(solution)/shard_map/dot_general | solution.py:22
  309.1 0.0 reduce-scatter.5.cloned.1.call-update
  309.1 0.0 reduce-scatter.7.cloned.1.call-start
  309.1 105.1 %reduce-scatter.5.cloned.1.call-done = bf16[384,3584]{1,0:T(8,128)(2,1)} async-done(((bf16[1536,3584]{1,0:T(8,128)(2,1)}), bf16[384,3584]{1,0:T(8,128)(2,1)}) %reduce-scatter.5.cloned.1.call-update) | async-done | bytes 2752528 | tf_op jit(solution)/shard_map/reduce_scatter | solution.py:53
  414.3 0.0 reduce-scatter.7.cloned.1.call-update
  414.3 0.0 reduce-scatter.9.cloned.1.call-start
  414.3 39.8 %reduce-scatter.7.cloned.1.call-done = bf16[96,3584]{1,0:T(8,128)(2,1)} async-done(((bf16[384,3584]{1,0:T(8,128)(2,1)}), bf16[96,3584]{1,0:T(8,128)(2,1)}) %reduce-scatter.7.cloned.1.call-update) | async-done | bytes 688144 | tf_op jit(solution)/shard_map/reduce_scatter | solution.py:53
  454.1 0.0 reduce-scatter.9.cloned.1.call-update
  454.1 0.0 reduce-scatter.11.cloned.1.call-start
  454.2 27.8 %reduce-scatter.9.cloned.1.call-done = bf16[24,3584]{1,0:T(8,128)(2,1)} async-done(((bf16[96,3584]{1,0:T(8,128)(2,1)}), bf16[24,3584]{1,0:T(8,128)(2,1)}) %reduce-scatter.9.cloned.1.call-update) | async-done | bytes 172048 | tf_op jit(solution)/shard_map/reduce_scatter | solution.py:53
  482.0 0.0 reduce-scatter.11.cloned.1.call-update
  482.0 25.7 %reduce-scatter.11.cloned.1.call-done = bf16[24,1792]{1,0:T(8,128)(2,1)} async-done(((bf16[24,3584]{1,0:T(8,128)(2,1)}), bf16[24,1792]{1,0:T(8,128)(2,1)}) %reduce-scatter.11.cloned.1.call-update) | async-done | bytes 86032 | tf_op jit(solution)/shard_map/reduce_scatter | solution.py:54
  507.7 0.9 copy.25
  508.6 4.1 all_to_all.19
  512.7 0.6 copy.27
  (3 shorter events, 0.0 us)
Async XLA Ops:
  6.5 178.0 %copy-start.1 = (s32[64]{0:T(128)S(1)}, s32[64]{0:T(128)}, u32[]{:S(2)}) copy-start(s32[64]{0:T(128)} %param.8) | copy-start | bytes 772
  6.5 178.0 %copy-start = (s32[64]{0:T(128)S(1)}, s32[64]{0:T(128)}, u32[]{:S(2)}) copy-start(s32[64]{0:T(128)} %param.9) | copy-start | bytes 772
  6.5 64.1 %all-gather.3.cloned.1.call-start = ((), (), s32[]{:S(2)}) async-start(), calls=%async_computation.5 | async-start | bytes 3563520 | tf_op jit(solution)/shard_map/all_gather | solution.py:43
  28.2 155.6 %all-gather.5.cloned.1.call-start = ((), (), s32[]{:S(2)}) async-start(), calls=%async_computation.6 | async-start | bytes 14254080 | tf_op jit(solution)/shard_map/all_gather | solution.py:43
  70.7 343.6 %reduce-scatter.5.cloned.1.call-start = ((), (), s32[]{:S(2)}) async-start(), calls=%async_computation.7 | async-start | bytes 13762560 | tf_op jit(solution)/shard_map/reduce_scatter | solution.py:53
  183.8 18.1 %collective-permute-start = (bf16[1536,3712]{1,0:T(8,128)(2,1)}, bf16[1536,3712]{1,0:T(8,128)(2,1)}, u32[]{:S(2)}, u32[]{:S(2)}) collective-permute-start(bf16[1536,3712]{1,0:T(8,128)(2,1)} %all-gather.5.cloned.1.call-done), channel_id=1, source_target_pairs={{0,1},{1,0},{2,3},{3,2},{4,5},{5,4},{6,7},{7,6},{8,9},{9,8},{10,11... | collective-permute-start | bytes 34209800 | tf_op jit(solution)/shard_map/ppermute | solution.py:44
  272.7 17.2 %collective-permute-start.1 = (bf16[1536,3584]{1,0:T(8,128)(2,1)}, bf16[1536,3584]{1,0:T(8,128)(2,1)}, u32[]{:S(2)}, u32[]{:S(2)}) collective-permute-start(bf16[1536,3584]{1,0:T(8,128)(2,1)} %multiply_convert_fusion), channel_id=1, source_target_pairs={{0,1},{1,0},{2,3},{3,2},{4,5},{5,4},{6,7},{7,6},{8,9},{9,8},{10,11... | collective-permute-start | bytes 33030152 | tf_op jit(solution)/shard_map/ppermute | solution.py:50
  309.1 145.0 %reduce-scatter.7.cloned.1.call-start = ((), (), s32[]{:S(2)}) async-start(), calls=%async_computation.8 | async-start | bytes 3440640 | tf_op jit(solution)/shard_map/reduce_scatter | solution.py:53
  414.3 67.7 %reduce-scatter.9.cloned.1.call-start = ((), (), s32[]{:S(2)}) async-start(), calls=%async_computation.9 | async-start | bytes 860160 | tf_op jit(solution)/shard_map/reduce_scatter | solution.py:53
  454.1 53.6 %reduce-scatter.11.cloned.1.call-start = ((), (), s32[]{:S(2)}) async-start(), calls=%async_computation.10 | async-start | bytes 258048 | tf_op jit(solution)/shard_map/reduce_scatter | solution.py:54
Sparse Core Ops, SparseCore 0:
  28.3 42.3 all-gather.2
  72.5 111.2 all-gather.4
  309.2 105.0 reduce-scatter.4
  416.7 37.3 reduce-scatter.6
  456.5 25.4 reduce-scatter.8
  484.4 23.2 reduce-scatter.10
where the time goes:
time: 520 us
  waiting for transfers between devices  380 us (73%)
  matrix products  49.5 us (10%)
  other arithmetic  48.9 us (9%)
  blocking collectives  23 us (4%)
  between operations  13.5 us (3%)
    reduce_scatter x3, waiting for transfers between devices, shards(): total = lax.psum_scatter(total, axis, scatter_dimension=0, tiled=True)  173 us
    all_gather x2, waiting for transfers between devices, shards(): own = lax.all_gather(own, axis, axis=0, tiled=True)  156 us
    reduce_sum x1, other arithmetic, expert_hidden(): jnp.sum(jnp.where((slots[:, :, None] == ids) & hit, weight[:, :, None], 0...  45.4 us
    dot_general x2, matrix products, down_project(): lax.dot_general(h, w_down, (((1,), (1,)), ((), ())), preferred_element_ty...  36.8 us
    reduce_scatter x1, waiting for transfers between devices, shards(): lax.psum_scatter(total.astype(jnp.float32), 'z_hi', scatter_dimension=1,...  25.7 us
    all_gather x1, blocking collectives, shards(): own = lax.all_gather(own, axis, axis=0, tiled=True)  18.9 us
    ppermute x1, waiting for transfers between devices, shards(): other = lax.ppermute(own, 'core', [(0, 1), (1, 0)])  15.7 us
    ppermute x1, waiting for transfers between devices, shards(): returned = lax.ppermute(away, 'core', [(0, 1), (1, 0)])  10.5 us
  transfers between devices with their start and end apart: 8, of which 8 were waited for; matrix products, arithmetic and copies ran while one was open for 2% of the time, Pallas kernels for 0%

commit v1 on v0

--- a/solution.py
+++ b/solution.py
@@ -40,7 +40,8 @@
     )
     own = lax.dynamic_slice_in_dim(packed, core * half, half, axis=0)
     for axis in GATHER_AXES:
-        own = lax.all_gather(own, axis, axis=0, tiled=True)
+        repeated = jnp.stack([own] * lax.axis_size(axis))
+        own = jnp.concatenate(lax.all_to_all(repeated, axis, 0, 0), axis=0)
     other = lax.ppermute(own, "core", [(0, 1), (1, 0)])
     hit = jnp.stack([partner, replica], axis=1).reshape(-1) == me
     w = expert_weights[0]

time: 520 us -> 543 us (1.044)
  blocking collectives: 23 us -> 197 us
  waiting for transfers between devices: 380 us -> 220 us
    all_to_all x0 -> x3, blocking collectives: none -> 193 us  [shards(): own = jnp.concatenate(lax.all_to_all(repeated, axis, 0, 0), axis=0)]
    all_gather x2 -> x0, waiting for transfers between devices: 156 us -> none  [shards(): own = lax.all_gather(own, axis, axis=0, tiled=True)]
    all_gather x1 -> x0, blocking collectives: 18.9 us -> none  [shards(): own = lax.all_gather(own, axis, axis=0, tiled=True)]
  transfers between devices with their start and end apart: 8 -> 6, of which waited for: 8 -> 6; matrix products, arithmetic and copies ran while one was open for 2% -> 1% of each run, Pallas kernels for 0% -> 0%
where the time goes in v1:
time: 543 us; the launch traced here: 542 us
  waiting for transfers between devices  220 us (41%)
  blocking collectives  197 us (36%)
  matrix products  49.5 us (9%)
  other arithmetic  48.9 us (9%)
  between operations  13.2 us (2%)
  local copies, waits for them, and re-layouts  8.95 us (2%)
    all_to_all x3, blocking collectives, shards(): own = jnp.concatenate(lax.all_to_all(repeated, axis, 0, 0), axis=0)  193 us
    reduce_scatter x3, waiting for transfers between devices, shards(): total = lax.psum_scatter(total, axis, scatter_dimension=0, tiled=True)  168 us
    reduce_sum x1, other arithmetic, expert_hidden(): jnp.sum(jnp.where((slots[:, :, None] == ids) & hit, weight[:, :, None], 0...  45.4 us
    dot_general x2, matrix products, down_project(): lax.dot_general(h, w_down, (((1,), (1,)), ((), ())), preferred_element_ty...  36.8 us
    reduce_scatter x1, waiting for transfers between devices, shards(): lax.psum_scatter(total.astype(jnp.float32), 'z_hi', scatter_dimension=1,...  26 us
    ppermute x1, waiting for transfers between devices, shards(): other = lax.ppermute(own, 'core', [(0, 1), (1, 0)])  15.6 us
  transfers between devices with their start and end apart: 6, of which 6 were waited for; matrix products, arithmetic and copies ran while one was open for 1% of the time, Pallas kernels for 0%

profile of v1, /device:TPU:1, one launch (start us, length us, event | category | flops | bytes accessed | tf_op | source)
XLA Modules:
  0.0 542.0 jit_solution(10374392510119692293)
XLA Ops:
  6.5 0.0 reduce-scatter.5.cloned.1.call-start
  6.5 0.7 convert_element_type.36
  7.2 0.1 copy.19
  7.3 0.8 copy.20
  8.1 1.1 concatenate.3
  9.3 24.2 %all_to_all.34 = bf16[4,24,3712]{2,1,0:T(8,128)(2,1)S(1)} all-to-all(bf16[4,24,3712]{2,1,0:T(8,128)(2,1)S(1)} %stack.22), channel_id=1, replica_groups=mesh['y'=4,'x'=4,'z_lo'=4,'z_hi'=2,'core'=2] {'z_lo'}, dimensions={0} | all-to-all | bytes 1425408 | tf_op jit(solution)/shard_map/all_to_all | solution.py:44
  33.5 0.2 stack.23
  33.7 36.3 %all_to_all.35 = bf16[4,96,3712]{2,1,0:T(8,128)(2,1)S(1)} all-to-all(bf16[4,96,3712]{2,1,0:T(8,128)(2,1)S(1)} %stack.23), channel_id=1, replica_groups=mesh['y'=4,'x'=4,'z_lo'=4,'z_hi'=2,'core'=2] {'y'}, dimensions={0} | all-to-all | bytes 5701632 | tf_op jit(solution)/shard_map/all_to_all | solution.py:44
  70.0 4.9 stack.24
  74.9 0.0 copy-start
  74.9 0.0 copy-start.1
  75.0 132.1 %all_to_all.36 = bf16[4,384,3712]{2,1,0:T(8,128)(2,1)} all-to-all(bf16[4,384,3712]{2,1,0:T(8,128)(2,1)} %stack.24), channel_id=1, replica_groups=mesh['y'=4,'x'=4,'z_lo'=4,'z_hi'=2,'core'=2] {'x'}, dimensions={0} | all-to-all | bytes 22806528 | tf_op jit(solution)/shard_map/all_to_all | solution.py:44
  207.1 3.9 collective-permute-start
  211.0 0.0 copy-done
  211.0 0.0 copy-done.1
  211.0 0.1 copy.21
  211.1 0.1 eq.44
  211.3 1.5 slice_convert_fusion.3
  212.8 15.6 %collective-permute-done = bf16[1536,3712]{1,0:T(8,128)(2,1)} collective-permute-done((bf16[1536,3712]{1,0:T(8,128)(2,1)}, bf16[1536,3712]{1,0:T(8,128)(2,1)}, u32[]{:S(2)}, u32[]{:S(2)}) %collective-permute-start) | collective-permute-done | bytes 11403296 | tf_op jit(solution)/shard_map/ppermute | solution.py:45
  228.4 1.3 slice_convert_fusion.1
  229.8 45.4 %select_reduce_fusion.1 = (f32[1536]{0:T(1024)S(1)}, f32[1536]{0:T(1024)S(1)}) fusion(f32[1536,8]{1,0:T(8,128)S(1)} %get-tuple-element.10, f32[1536,8]{1,0:T(8,128)S(1)} %get-tuple-element.9, pred[128]{0:T(512)(128)(4,1)S(1)} %eq.44, f32[1536,8]{1,0:T(8,128)S(1)} %get-tuple-element.8, f32[1536,8]{1,0:T(8,128)S(1)} %get-tuple-element.7), kind=kLoop, calls=%fused_computation.12 | loop fusion | flops 12579840 | bytes 209024 | tf_op jit(solution)/shard_map/reduce_sum | solution.py:15
  275.1 6.3 %fusion = f32[1536,256]{1,0:T(8,128)S(1)} fusion(bf16[1536,3712]{1,0:T(8,128)(2,1)} %collective-permute-done, bf16[1,3,3584,256]{3,2,1,0:T(8,128)(2,1)} %param.7), kind=kOutput, calls=%fused_computation.2 | convolution fusion | flops 2818572288 | bytes 14417920 | tf_op jit(solution)/shard_map/dot_general | solution.py:17
  281.5 17.6 %multiply_convert_fusion = bf16[1536,3584]{1,0:T(8,128)(2,1)} fusion(f32[1536]{0:T(1024)S(1)} %get-tuple-element.6, bf16[1,3,3584,256]{3,2,1,0:T(8,128)(2,1)} %param.7, f32[1536,256]{1,0:T(8,128)S(1)} %fusion, bf16[1536,3712]{1,0:T(8,128)(2,1)} %collective-permute-done), kind=kOutput, calls=%fused_computation.1 | convolution fusion | flops 5650513920 | bytes 27269120 | tf_op jit(solution)/shard_map/dot_general | solution.py:22
  299.1 0.4 collective-permute-start.1
  299.5 6.3 %fusion.6 = f32[1536,256]{1,0:T(8,128)S(1)} fusion(bf16[1536,3712]{1,0:T(8,128)(2,1)} %bitcast.2, bf16[1,3,3584,256]{3,2,1,0:T(8,128)(2,1)} %param.7), kind=kOutput, calls=%fused_computation.8 | convolution fusion | flops 2818572288 | bytes 14417920 | tf_op jit(solution)/shard_map/dot_general | solution.py:16
  305.8 10.5 %collective-permute-done.1 = bf16[1536,3584]{1,0:T(8,128)(2,1)} collective-permute-done((bf16[1536,3584]{1,0:T(8,128)(2,1)}, bf16[1536,3584]{1,0:T(8,128)(2,1)}, u32[]{:S(2)}, u32[]{:S(2)}) %collective-permute-start.1) | collective-permute-done | bytes 11010080 | tf_op jit(solution)/shard_map/ppermute | solution.py:51
  316.4 19.1 %add_convert_fusion = bf16[1536,3584]{1,0:T(8,128)(2,1)} fusion(bf16[1536,3584]{1,0:T(8,128)(2,1)} %collective-permute-done.1, f32[1536]{0:T(1024)S(1)} %get-tuple-element.5, bf16[1536,3712]{1,0:T(8,128)(2,1)} %bitcast.2, bf16[1,3,3584,256]{3,2,1,0:T(8,128)(2,1)} %param.7, f32[1536,256]{1,0:T(8,128)S(1)} %fusion.6), kind=kOutput, calls=%fused_computation | convolution fusion | flops 5661523968 | bytes 38279168 | tf_op jit(solution)/shard_map/dot_general | solution.py:22
  335.5 0.0 reduce-scatter.5.cloned.1.call-update
  335.6 0.0 reduce-scatter.7.cloned.1.call-start
  335.6 100.5 %reduce-scatter.5.cloned.1.call-done = bf16[384,3584]{1,0:T(8,128)(2,1)} async-done(((bf16[1536,3584]{1,0:T(8,128)(2,1)}), bf16[384,3584]{1,0:T(8,128)(2,1)}) %reduce-scatter.5.cloned.1.call-update) | async-done | bytes 2752528 | tf_op jit(solution)/shard_map/reduce_scatter | solution.py:54
  436.1 0.0 reduce-scatter.7.cloned.1.call-update
  436.1 0.0 reduce-scatter.9.cloned.1.call-start
  436.2 39.9 %reduce-scatter.7.cloned.1.call-done = bf16[96,3584]{1,0:T(8,128)(2,1)} async-done(((bf16[384,3584]{1,0:T(8,128)(2,1)}), bf16[96,3584]{1,0:T(8,128)(2,1)}) %reduce-scatter.7.cloned.1.call-update) | async-done | bytes 688144 | tf_op jit(solution)/shard_map/reduce_scatter | solution.py:54
  476.1 0.0 reduce-scatter.9.cloned.1.call-update
  476.1 0.0 reduce-scatter.11.cloned.1.call-start
  476.2 27.7 %reduce-scatter.9.cloned.1.call-done = bf16[24,3584]{1,0:T(8,128)(2,1)} async-done(((bf16[96,3584]{1,0:T(8,128)(2,1)}), bf16[24,3584]{1,0:T(8,128)(2,1)}) %reduce-scatter.9.cloned.1.call-update) | async-done | bytes 172048 | tf_op jit(solution)/shard_map/reduce_scatter | solution.py:54
  503.8 0.0 reduce-scatter.11.cloned.1.call-update
  503.8 26.0 %reduce-scatter.11.cloned.1.call-done = bf16[24,1792]{1,0:T(8,128)(2,1)} async-done(((bf16[24,3584]{1,0:T(8,128)(2,1)}), bf16[24,1792]{1,0:T(8,128)(2,1)}) %reduce-scatter.11.cloned.1.call-update) | async-done | bytes 86032 | tf_op jit(solution)/shard_map/reduce_scatter | solution.py:55
  529.9 0.9 copy.25
  530.8 4.1 all_to_all.37
  534.8 0.6 copy.27
  (4 shorter events, 0.1 us)
Async XLA Ops:
  6.5 429.6 %reduce-scatter.5.cloned.1.call-start = ((), (), s32[]{:S(2)}) async-start(), calls=%async_computation.8 | async-start | bytes 13762560 | tf_op jit(solution)/shard_map/reduce_scatter | solution.py:54
  74.9 136.1 %copy-start = (s32[64]{0:T(128)S(1)}, s32[64]{0:T(128)}, u32[]{:S(2)}) copy-start(s32[64]{0:T(128)} %param.9) | copy-start | bytes 772
  74.9 136.1 %copy-start.1 = (s32[64]{0:T(128)S(1)}, s32[64]{0:T(128)}, u32[]{:S(2)}) copy-start(s32[64]{0:T(128)} %param.8) | copy-start | bytes 772
  207.1 21.4 %collective-permute-start = (bf16[1536,3712]{1,0:T(8,128)(2,1)}, bf16[1536,3712]{1,0:T(8,128)(2,1)}, u32[]{:S(2)}, u32[]{:S(2)}) collective-permute-start(bf16[1536,3712]{1,0:T(8,128)(2,1)} %bitcast.2), channel_id=1, source_target_pairs={{0,1},{1,0},{2,3},{3,2},{4,5},{5,4},{6,7},{7,6},{8,9},{9,8},{10,11... | collective-permute-start | bytes 34209800 | tf_op jit(solution)/shard_map/ppermute | solution.py:45
  299.1 17.2 %collective-permute-start.1 = (bf16[1536,3584]{1,0:T(8,128)(2,1)}, bf16[1536,3584]{1,0:T(8,128)(2,1)}, u32[]{:S(2)}, u32[]{:S(2)}) collective-permute-start(bf16[1536,3584]{1,0:T(8,128)(2,1)} %multiply_convert_fusion), channel_id=1, source_target_pairs={{0,1},{1,0},{2,3},{3,2},{4,5},{5,4},{6,7},{7,6},{8,9},{9,8},{10,11... | collective-permute-start | bytes 33030152 | tf_op jit(solution)/shard_map/ppermute | solution.py:51
  335.6 140.5 %reduce-scatter.7.cloned.1.call-start = ((), (), s32[]{:S(2)}) async-start(), calls=%async_computation.9 | async-start | bytes 3440640 | tf_op jit(solution)/shard_map/reduce_scatter | solution.py:54
  436.1 67.7 %reduce-scatter.9.cloned.1.call-start = ((), (), s32[]{:S(2)}) async-start(), calls=%async_computation.10 | async-start | bytes 860160 | tf_op jit(solution)/shard_map/reduce_scatter | solution.py:54
  476.1 53.8 %reduce-scatter.11.cloned.1.call-start = ((), (), s32[]{:S(2)}) async-start(), calls=%async_computation.11 | async-start | bytes 258048 | tf_op jit(solution)/shard_map/reduce_scatter | solution.py:55
Sparse Core Ops, SparseCore 0:
  335.7 100.3 reduce-scatter.4
  438.7 37.3 reduce-scatter.6
  478.6 25.1 reduce-scatter.8
  506.3 23.5 reduce-scatter.10
